TPU v7x, 512 devices: a whole 4x4x16 slice. The times are simulated.
512 devices in a mesh: grp: 32 (over y, x, core), sub: 16 (over z).
Axes of the slice: x: 4, y: 4, z: 16, core: 2. Of those that a mesh axis runs over, the one named last changes fastest.
Arguments:
- loads: bfloat16 [32, 16, 16, 1536], P('grp', 'sub'), may hold values from -6 to 6
- boundary_values: float32 [16, 6144], replicated, may hold values from -6 to 6
- dirichlet_ids: int32 [32, 16, 3, 128], P('grp', 'sub'), may hold values from 0 to 6143
- dirichlet_coupling: bfloat16 [32, 16, 3, 512, 128], P('grp', 'sub'), may hold values from -0.5 to 0.5
- local_inverse: bfloat16 [32, 16, 3, 512, 512], P('grp', 'sub'), as said below
- local_schur: bfloat16 [32, 16, 3, 512, 512], P('grp', 'sub')
- corner_coupling: bfloat16 [32, 16, 3, 24, 512], P('grp', 'sub'), may hold values from -0.25 to 0.25
- corner_ids: int32 [32, 16, 3, 24], P('grp', 'sub'), may hold values from 0 to 12287
- coarse_inverse: bfloat16 [12288, 12288], P(('grp', 'sub')), as said below
- row_counts: int32 [32, 16, 18], P('grp', 'sub'), may hold values from 0 to 256, as said below
- slot_of: int32 [32, 16, 1536], P('grp', 'sub'), may hold values from 0 to 1535, each once within a row
Outputs:
- multipliers: float32 [32, 16, 16, 1536], P('grp', 'sub')
- residual: float32 [32, 16, 16, 1536], P('grp', 'sub')
Inputs may be any that keep to these rules, and one draw needn't show every extreme that they name: row_counts[g, s, p] for p < 16 equals row_counts[g, p, s], is 0 for p = s and lies in 1 to 64 otherwise; every device reaches 64 with some peer. Column 16 of device (g, s) equals column 17 of device (g - 1, s), lies in 1 to 256, reaches 256 on some device of every slab boundary, and is 0 in the first slab; column 17 is 0 in the last slab. coarse_inverse is symmetric and positive definite. local_inverse and local_schur are symmetric and positive definite.
All inputs are finite; a program needn't handle non-finite values.
Results may differ from a plain program's by a relative error of at most 0.012.
Values may be sent and summed in bfloat16 or wider, within the bound.
No kernel may reach another device: no remote copies, remote signals or barrier semaphores. Data moves between devices by JAX's collectives and lax.ppermute only.
A program may use at most 64 MiB of HBM per device.

v0:
```python
import jax
import jax.numpy as jnp
from jax import lax
from jax.sharding import PartitionSpec as P

IFACE = 512
SUBS_DEV = 3
LOADS = 16
CORNERS = 24
SLAB_ROWS = 256
ITERS = 2


def extended(cells, sides, width):
    for axis, dim in sides:
        count = lax.axis_size(axis)
        ends = count - 1
        head = lax.slice_in_dim(cells, 0, width, axis=dim)
        tail = lax.slice_in_dim(cells, cells.shape[dim] - width, cells.shape[dim], axis=dim)
        cells = jnp.concatenate(
            [
                lax.ppermute(tail, axis, [(i, (i + 1) % count) for i in range(ends)]),
                cells,
                lax.ppermute(head, axis, [((i + 1) % count, i) for i in range(ends)]),
            ],
            axis=dim,
        )
    return cells


def per_device(
    loads,
    boundary_values,
    dirichlet_ids,
    dirichlet_coupling,
    local_inverse,
    local_schur,
    corner_coupling,
    corner_ids,
    coarse_inverse,
    row_counts,
    slot_of,
):
    load_cases = loads[0, 0]
    fixed_ids = dirichlet_ids[0, 0]
    fixed_coupling = dirichlet_coupling[0, 0]
    inverse_blocks = local_inverse[0, 0]
    schur_blocks = local_schur[0, 0]
    coupling = corner_coupling[0, 0]
    corner_index = corner_ids[0, 0].reshape(-1)
    counts = row_counts[0, 0]
    slots = slot_of[0, 0]
    n_sub = lax.axis_size("sub")
    length = slots.shape[0]
    peer_rows = (length - 2 * SLAB_ROWS) // n_sub
    within = n_sub * peer_rows
    coarse_size = coarse_inverse.shape[1]
    positions = jnp.arange(length, dtype=jnp.int32)
    slot_inverse = jnp.zeros(length, jnp.int32).at[slots].set(positions)
    column = jnp.where(
        positions < within, positions // peer_rows, n_sub + (positions - within) // SLAB_ROWS
    )
    offset = jnp.where(positions < within, positions % peer_rows, (positions - within) % SLAB_ROWS)
    canon_live = (offset < counts[column]).astype(jnp.float32)
    live_mask = canon_live[slot_inverse][None, :]
    peer_index = slots[:within].reshape(n_sub, peer_rows)
    slab_index = slots[within:].reshape(2, SLAB_ROWS)

    def partner(values):
        outgoing = jnp.take(values, peer_index, axis=1)
        incoming = lax.all_to_all(outgoing, "sub", split_axis=1, concat_axis=1, tiled=True).reshape(
            LOADS, within
        )
        slab_part = jnp.take(values, slab_index, axis=1)
        padded = extended(slab_part, (("grp", 1),), 1)
        joined = jnp.concatenate([incoming, padded[:, 0], padded[:, 3]], axis=1)
        return jnp.take(joined, slot_inverse, axis=1)

    def apply_tilde(field_b):
        blocks = field_b.reshape(LOADS, SUBS_DEV, IFACE)
        local_part = jnp.einsum(
            "anm,ram->ran", inverse_blocks, blocks, preferred_element_type=jnp.float32
        )
        corner_terms = jnp.einsum(
            "acm,ram->rac", coupling, blocks, preferred_element_type=jnp.float32
        )
        partial_load = (
            jnp.zeros((LOADS, coarse_size), jnp.float32)
            .at[:, corner_index]
            .add(corner_terms.reshape(LOADS, -1))
        )
        coarse_load = lax.psum(partial_load, ("grp", "sub"))
        owned_values = jnp.einsum(
            "rj,ij->ri",
            coarse_load.astype(jnp.bfloat16),
            coarse_inverse,
            preferred_element_type=jnp.float32,
        )
        coarse_values = lax.all_gather(owned_values, ("grp", "sub"), axis=1, tiled=True)
        at_corners = (
            jnp.take(coarse_values, corner_index, axis=1)
            .astype(jnp.bfloat16)
            .reshape(LOADS, SUBS_DEV, CORNERS)
        )
        correction = jnp.einsum(
            "acm,rac->ram", coupling, at_corners, preferred_element_type=jnp.float32
        )
        return (local_part + correction).reshape(LOADS, length)

    def jumps(values):
        return live_mask * (values - partner(values))

    picked = jnp.take(boundary_values, fixed_ids, axis=1).astype(jnp.bfloat16)
    lifted_part = jnp.einsum(
        "and,rad->ran", fixed_coupling, picked, preferred_element_type=jnp.float32
    ).reshape(LOADS, length)
    lifted = live_mask * (load_cases.astype(jnp.float32) - lifted_part)
    jump_field = jumps(apply_tilde(lifted.astype(jnp.bfloat16)))
    multipliers = jnp.zeros_like(jump_field)
    residual = jump_field
    search = jump_field
    inner_before = jnp.ones((LOADS,), jnp.float32)
    for step in range(ITERS):
        smoothed = jnp.einsum(
            "anm,ram->ran",
            schur_blocks,
            residual.astype(jnp.bfloat16).reshape(LOADS, SUBS_DEV, IFACE),
            preferred_element_type=jnp.float32,
        ).reshape(LOADS, length)
        precond = 0.25 * live_mask * (smoothed - partner(smoothed))
        inner_now = lax.psum(jnp.sum(residual * precond, axis=1), ("grp", "sub"))
        if step == 0:
            search = precond
        else:
            search = precond + (inner_now / inner_before)[:, None] * search
        tilde = apply_tilde(search.astype(jnp.bfloat16))
        image = jumps(tilde)
        curvature = lax.psum(jnp.sum(search * image, axis=1), ("grp", "sub"))
        step_size = (inner_now / curvature)[:, None]
        multipliers = multipliers + step_size * search
        residual = residual - step_size * image
        inner_before = inner_now
    return (multipliers[None, None], residual[None, None])


def solution(mesh):
    in_specs = (
        P("grp", "sub", None, None),
        P(),
        P("grp", "sub", None, None),
        P("grp", "sub", None, None, None),
        P("grp", "sub", None, None, None),
        P("grp", "sub", None, None, None),
        P("grp", "sub", None, None, None),
        P("grp", "sub", None, None),
        P(("grp", "sub"), None),
        P("grp", "sub", None),
        P("grp", "sub", None),
    )
    out_specs = (P("grp", "sub", None, None), P("grp", "sub", None, None))
    return jax.shard_map(
        per_device, mesh=mesh, in_specs=in_specs, out_specs=out_specs, check_vma=False
    )
```

profile of v0, /device:TPU:1, one launch (start us, length us, event | category | flops | bytes accessed | tf_op | source)
XLA Modules:
  0.0 1553.7 jit_solution(18050115892917891328)
XLA Ops:
  7.5 6.2 scatter_custom_fusion
  13.8 2.0 fusion.121
  15.8 4.4 fusion.102
  20.2 6.9 fusion.100
  27.2 8.4 gather_fusion
  35.7 1.7 copy.263
  40.5 4.0 scatter_custom_fusion.1
  44.5 195.8 %all-reduce.4 = bf16[16,12288]{0,1:T(8,128)(2,1)} all-reduce(f32[16,12288]{0,1:T(8,128)} %scatter_custom_fusion.1), channel_id=1, replica_groups=mesh['grp'=32,'sub'=16] {'grp','sub'}, use_global_device_ids=true, to_apply=%region_2.3 | all-reduce | flops 196608 | bytes 1179648 | tf_op jit(solution)/shard_map/psum | solution.py:92
  240.3 2.8 fusion.49
  243.1 120.0 %all-gather = bf16[512,24,16]{1,2,0:T(8,128)(2,1)} all-gather(bf16[1,24,16]{1,2,0:T(8,128)(2,1)S(1)} %fusion.49), channel_id=1, replica_groups=mesh['grp'=32,'sub'=16] {'grp','sub'}, dimensions={0}, use_global_device_ids=true | all-gather | bytes 393984 | tf_op jit(solution)/shard_map/all_gather | solution.py:99
  363.1 4.5 copy.330
  367.6 3.0 gather_fusion.2
  372.6 4.0 gather_fusion.3
  378.6 1.7 reshape.762
  380.3 6.2 all-to-all-start
  387.3 2.8 gather_fusion.4
  391.8 8.2 collective-permute-start
  400.0 3.3 collective-permute-start.1
  411.1 4.8 gather_fusion.5
  419.6 2.8 gather_fusion.7
  422.4 5.1 gather_fusion.6
  429.4 1.7 reshape.764
  432.2 11.8 all-to-all-start.1
  444.5 2.7 collective-permute-start.2
  447.3 1.9 collective-permute-start.3
  449.2 7.0 all-to-all-done.1
  462.8 4.8 gather_fusion.8
  467.6 2.0 copy.287
  470.9 4.0 scatter_custom_fusion.2
  474.8 190.3 %all-reduce.5 = bf16[16,12288]{0,1:T(8,128)(2,1)} all-reduce(f32[16,12288]{0,1:T(8,128)} %scatter_custom_fusion.2), channel_id=1, replica_groups=mesh['grp'=32,'sub'=16] {'grp','sub'}, use_global_device_ids=true, to_apply=%region_6.11 | all-reduce | flops 196608 | bytes 1179648 | tf_op jit(solution)/shard_map/psum | solution.py:92
  665.1 3.0 fusion.52
  668.1 120.7 %all-gather.1 = bf16[512,24,16]{1,2,0:T(8,128)(2,1)} all-gather(bf16[1,24,16]{1,2,0:T(8,128)(2,1)S(1)} %fusion.52), channel_id=1, replica_groups=mesh['grp'=32,'sub'=16] {'grp','sub'}, dimensions={0}, use_global_device_ids=true | all-gather | bytes 393984 | tf_op jit(solution)/shard_map/all_gather | solution.py:99
  788.8 4.5 copy.331
  793.3 3.0 gather_fusion.9
  798.3 2.8 gather_fusion.11
  801.1 5.1 gather_fusion.10
  808.7 1.7 reshape.766
  811.4 6.2 all-to-all-start.2
  819.0 8.2 collective-permute-start.4
  827.2 3.7 collective-permute-start.5
  837.6 5.1 gather_fusion.12
  845.1 107.2 %all-reduce = (f32[16]{0:T(128)S(1)}, f32[16]{0:T(128)S(1)}) all-reduce(f32[16]{0:T(128)S(1)} %get-tuple-element.15, f32[16]{0:T(128)S(1)} %get-tuple-element.14), channel_id=1, replica_groups=mesh['grp'=32,'sub'=16] {'grp','sub'}, use_global_device_ids=true, to_apply=%region_4.9 | all-reduce | flops 32 | bytes 256 | tf_op jit(solution)/shard_map/psum | solution.py:131
  954.8 1.6 gather_fusion.14
  956.4 2.8 gather_fusion.13
  961.3 8.2 all-to-all-start.3
  970.2 2.8 collective-permute-start.6
  973.0 1.9 collective-permute-start.7
  974.9 6.2 all-to-all-done.3
  982.4 3.7 gather_fusion.15
  987.6 101.6 %psum.53 = f32[16]{0:T(128)S(1)} all-reduce(f32[16]{0:T(128)S(1)} %multiply_reduce_fusion.1), channel_id=1, replica_groups=mesh['grp'=32,'sub'=16] {'grp','sub'}, use_global_device_ids=true, to_apply=%region_10.15 | all-reduce | flops 16 | bytes 128 | tf_op jit(solution)/shard_map/psum | solution.py:131
  1090.3 4.0 scatter_custom_fusion.3
  1094.2 185.3 %all-reduce.6 = bf16[16,12288]{0,1:T(8,128)(2,1)} all-reduce(f32[16,12288]{0,1:T(8,128)} %scatter_custom_fusion.3), channel_id=1, replica_groups=mesh['grp'=32,'sub'=16] {'grp','sub'}, use_global_device_ids=true, to_apply=%region_12.17 | all-reduce | flops 196608 | bytes 1179648 | tf_op jit(solution)/shard_map/psum | solution.py:92
  1279.5 2.8 fusion.55
  1282.3 120.6 %all-gather.2 = bf16[512,24,16]{1,2,0:T(8,128)(2,1)} all-gather(bf16[1,24,16]{1,2,0:T(8,128)(2,1)S(1)} %fusion.55), channel_id=1, replica_groups=mesh['grp'=32,'sub'=16] {'grp','sub'}, dimensions={0}, use_global_device_ids=true | all-gather | bytes 393984 | tf_op jit(solution)/shard_map/all_gather | solution.py:99
  1403.0 4.5 copy.332
  1407.5 3.0 gather_fusion.16
  1411.6 1.6 gather_fusion.18
  1413.2 2.8 gather_fusion.17
  1418.1 8.8 all-to-all-start.4
  1426.9 8.2 collective-permute-start.8
  1435.1 3.1 collective-permute-start.9
  1440.8 2.6 gather_fusion.19
  1444.6 107.4 %psum.55 = f32[16]{0:T(128)S(1)} all-reduce(f32[16]{0:T(128)S(1)} %multiply_reduce_fusion), channel_id=1, replica_groups=mesh['grp'=32,'sub'=16] {'grp','sub'}, use_global_device_ids=true, to_apply=%region_14.19 | all-reduce | flops 16 | bytes 128 | tf_op jit(solution)/shard_map/psum | solution.py:138
  1552.0 1.7 subtract_bitcast_fusion
  (234 shorter events, 71.2 us)
Async XLA Ops:
  0.6 370.3 %copy-start = (bf16[1,1,3,512,512]{4,3,2,1,0:T(8,128)(2,1)S(1)}, bf16[1,1,3,512,512]{4,3,2,1,0:T(8,128)(2,1)}, u32[]{:S(2)}) copy-start(bf16[1,1,3,512,512]{4,3,2,1,0:T(8,128)(2,1)} %param.23) | copy-start | bytes 4718596
  5.5 423.2 %copy-start.15 = (pred[16,64]{1,0:T(8,128)(4,1)}, pred[16,64]{1,0:T(8,128)(4,1)S(1)}, u32[]{:S(2)}) copy-start(pred[16,64]{1,0:T(8,128)(4,1)S(1)} %compare_and_fusion.1) | copy-start | bytes 3076
  7.5 793.5 %copy-start.7 = (s32[1024]{0:T(1024)}, s32[1024]{0:T(1024)S(1)}, u32[]{:S(2)}) copy-start(s32[1024]{0:T(1024)S(1)} %broadcast_clamp_fusion) | copy-start | bytes 12292
  13.7 21.8 %copy-start.17 = (s32[1536]{0:T(1024)}, s32[1536]{0:T(1024)S(1)}, u32[]{:S(2)}) copy-start(s32[1536]{0:T(1024)S(1)} %scatter_custom_fusion) | copy-start | bytes 18436
  13.7 449.1 %copy-start.9 = (s32[2048]{0:T(1024)}, s32[2048]{0:T(1024)S(1)}, u32[]{:S(2)}) copy-start(s32[2048]{0:T(1024)S(1)} %pad_clamp_fusion) | copy-start | bytes 24580
  27.1 8.5 copy-start.22
  27.1 11.8 copy-start.29
  27.1 13.0 copy-start.5
  44.5 195.8 %copy-start.3 = (bf16[24,12288]{1,0:T(8,128)(2,1)S(1)}, bf16[24,12288]{1,0:T(8,128)(2,1)}, u32[]{:S(2)}) copy-start(bf16[24,12288]{1,0:T(8,128)(2,1)} %param.27) | copy-start | bytes 1769476
  363.1 7.5 copy-start.26
  371.7 0.9 copy-start.2
  376.6 41.3 %copy-start.1 = (bf16[1,1,3,512,512]{4,3,2,1,0:T(8,128)(2,1)S(1)}, bf16[1,1,3,512,512]{4,3,2,1,0:T(8,128)(2,1)}, u32[]{:S(2)}) copy-start(bf16[1,1,3,512,512]{4,3,2,1,0:T(8,128)(2,1)} %param.24) | copy-start | bytes 4718596
  380.3 23.6 %all-to-all-start = ((f32[16,1,1024]{2,1,0:T(1,128)}), f32[16,1,1024]{2,1,0:T(1,128)S(1)}, u32[]{:S(2)}, u32[]{:S(2)}) async-start(f32[16,1,1024]{2,1,0:T(1,128)} %reshape.762), calls=%async_computation | async-start | bytes 131072 | tf_op jit(solution)/shard_map/all_to_all | solution.py:71
  387.2 28.7 %copy-start.23 = (pred[2,256]{1,0:T(4,128)(4,1)}, pred[2,256]{1,0:T(4,128)(4,1)S(1)}, u32[]{:S(2)}) copy-start(pred[2,256]{1,0:T(4,128)(4,1)S(1)} %compare_and_fusion.2) | copy-start | bytes 1540
  387.3 2.8 copy-start.18
  391.8 17.4 %collective-permute-start = (f32[16,1,256]{2,0,1:T(8,128)}, f32[16,1,256]{2,0,1:T(8,128)S(1)}, u32[]{:S(2)}, u32[]{:S(2)}) collective-permute-start(f32[16,1,256]{2,0,1:T(8,128)} %get-tuple-element.34), channel_id=1, source_target_pairs={{0,16},{16,32},{32,48},{48,64},{64,80},{80,96},{96,112},{112,128},... | collective-permute-start | bytes 49160 | tf_op jit(solution)/shard_map/ppermute | solution.py:22
  400.0 9.2 collective-permute-start.1
  403.9 65.7 %copy-start.11 = (pred[1536]{0:T(1024)(128)(4,1)}, pred[1536]{0:T(1024)(128)(4,1)S(1)}, u32[]{:S(2)}) copy-start(pred[1536]{0:T(1024)(128)(4,1)S(1)} %compare_and_fusion) | copy-start | bytes 4612
  407.5 12.2 copy-start.19
  418.5 13.7 copy-start.24
  432.2 24.0 %all-to-all-start.1 = ((f32[16,1,1024]{2,1,0:T(1,128)}), f32[16,1,1024]{2,1,0:T(1,128)S(1)}, u32[]{:S(2)}, u32[]{:S(2)}) async-start(f32[16,1,1024]{2,1,0:T(1,128)} %reshape.764), calls=%async_computation.1 | async-start | bytes 131072 | tf_op jit(solution)/shard_map/all_to_all | solution.py:71
  444.5 16.3 %collective-permute-start.2 = (f32[16,1,256]{2,0,1:T(8,128)}, f32[16,1,256]{2,0,1:T(8,128)S(1)}, u32[]{:S(2)}, u32[]{:S(2)}) collective-permute-start(f32[16,1,256]{2,0,1:T(8,128)} %get-tuple-element.32), channel_id=1, source_target_pairs={{0,16},{16,32},{32,48},{48,64},{64,80},{80,96},{96,112},{112,128},... | collective-permute-start | bytes 49160 | tf_op jit(solution)/shard_map/ppermute | solution.py:22
  447.3 13.5 collective-permute-start.3
  449.2 25.7 %copy-start.13 = (f32[1536]{0:T(1024)}, f32[1536]{0:T(1024)S(1)}, u32[]{:S(2)}) copy-start(f32[1536]{0:T(1024)S(1)} %broadcast_multiply_fusion) | copy-start | bytes 18436
  788.8 7.5 copy-start.27
  788.8 9.5 copy-start.20
  811.4 19.4 %all-to-all-start.2 = ((f32[16,1,1024]{2,1,0:T(1,128)}), f32[16,1,1024]{2,1,0:T(1,128)S(1)}, u32[]{:S(2)}, u32[]{:S(2)}) async-start(f32[16,1,1024]{2,1,0:T(1,128)} %reshape.766), calls=%async_computation.2 | async-start | bytes 131072 | tf_op jit(solution)/shard_map/all_to_all | solution.py:71
  819.0 16.5 %collective-permute-start.4 = (f32[16,1,256]{2,0,1:T(8,128)}, f32[16,1,256]{2,0,1:T(8,128)}, u32[]{:S(2)}, u32[]{:S(2)}) collective-permute-start(f32[16,1,256]{2,0,1:T(8,128)} %get-tuple-element.30), channel_id=1, source_target_pairs={{0,16},{16,32},{32,48},{48,64},{64,80},{80,96},{96,112},{112,128},... | collective-permute-start | bytes 49160 | tf_op jit(solution)/shard_map/ppermute | solution.py:22
  827.2 8.3 collective-permute-start.5
  833.9 118.4 %copy-start.12 = (pred[1536]{0:T(1024)(128)(4,1)S(1)}, pred[1536]{0:T(1024)(128)(4,1)}, u32[]{:S(2)}) copy-start(pred[1536]{0:T(1024)(128)(4,1)} %copy-done.11) | copy-start | bytes 4612
  836.4 118.4 %copy-start.21 = (s32[1024]{0:T(1024)S(1)}, s32[1024]{0:T(1024)}, u32[]{:S(2)}) copy-start(s32[1024]{0:T(1024)} %copy-done.18) | copy-start | bytes 12292
  836.4 120.0 %copy-start.8 = (s32[1024]{0:T(1024)S(1)}, s32[1024]{0:T(1024)}, u32[]{:S(2)}) copy-start(s32[1024]{0:T(1024)} %copy-done.7) | copy-start | bytes 12292
  842.7 116.8 %copy-start.16 = (pred[16,64]{1,0:T(8,128)(4,1)S(1)}, pred[16,64]{1,0:T(8,128)(4,1)}, u32[]{:S(2)}) copy-start(pred[16,64]{1,0:T(8,128)(4,1)} %copy-done.15) | copy-start | bytes 3076
  952.3 2.4 copy-start.34
  952.3 1.6 copy-start.30
  954.5 28.0 %copy-start.10 = (s32[2048]{0:T(1024)S(1)}, s32[2048]{0:T(1024)}, u32[]{:S(2)}) copy-start(s32[2048]{0:T(1024)} %copy-done.9) | copy-start | bytes 24580
  956.4 31.0 %copy-start.6 = (f32[16,1536]{1,0:T(8,128)S(1)}, f32[16,1536]{1,0:T(8,128)}, u32[]{:S(2)}) copy-start(f32[16,1536]{1,0:T(8,128)} %get-tuple-element.21) | copy-start | bytes 294916
  956.4 31.0 %copy-start.14 = (f32[1536]{0:T(1024)S(1)}, f32[1536]{0:T(1024)}, u32[]{:S(2)}) copy-start(f32[1536]{0:T(1024)} %copy-done.13) | copy-start | bytes 18436
  956.4 132.8 %copy-start.35 = (f32[16]{0:T(128)S(1)}, f32[16]{0:T(128)}, u32[]{:S(2)}) copy-start(f32[16]{0:T(128)} %copy-done.34) | copy-start | bytes 196
  961.3 19.8 %all-to-all-start.3 = ((f32[16,1,1024]{2,1,0:T(1,128)}), f32[16,1,1024]{2,1,0:T(1,128)S(1)}, u32[]{:S(2)}, u32[]{:S(2)}) async-start(f32[16,1,1024]{2,1,0:T(1,128)} %reshape.768), calls=%async_computation.3 | async-start | bytes 131072 | tf_op jit(solution)/shard_map/all_to_all | solution.py:71
  970.2 11.9 collective-permute-start.6
  973.0 9.1 collective-permute-start.7
  1089.2 5.0 copy-start.32
  1094.2 185.3 %copy-start.4 = (bf16[24,12288]{1,0:T(8,128)(2,1)S(1)}, bf16[24,12288]{1,0:T(8,128)(2,1)}, u32[]{:S(2)}) copy-start(bf16[24,12288]{1,0:T(8,128)(2,1)} %param.27) | copy-start | bytes 1769476
  1403.0 7.5 copy-start.28
  1407.5 19.4 %copy-start.25 = (pred[2,256]{1,0:T(4,128)(4,1)S(1)}, pred[2,256]{1,0:T(4,128)(4,1)}, u32[]{:S(2)}) copy-start(pred[2,256]{1,0:T(4,128)(4,1)} %copy-done.23) | copy-start | bytes 1540
  1413.2 138.8 %copy-start.33 = (f32[16]{0:T(128)S(1)}, f32[16]{0:T(128)}, u32[]{:S(2)}) copy-start(f32[16]{0:T(128)} %copy-done.32) | copy-start | bytes 196
  1413.2 138.8 %copy-start.31 = (f32[16]{0:T(128)S(1)}, f32[16]{0:T(128)}, u32[]{:S(2)}) copy-start(f32[16]{0:T(128)} %copy-done.30) | copy-start | bytes 196
  1418.1 20.4 %all-to-all-start.4 = ((f32[16,1,1024]{2,1,0:T(1,128)}), f32[16,1,1024]{2,1,0:T(1,128)S(1)}, u32[]{:S(2)}, u32[]{:S(2)}) async-start(f32[16,1,1024]{2,1,0:T(1,128)} %reshape.770), calls=%async_computation.4 | async-start | bytes 131072 | tf_op jit(solution)/shard_map/all_to_all | solution.py:71
  1426.9 12.6 collective-permute-start.8
  1435.1 5.4 collective-permute-start.9
where the time goes:
time: 1560 us; the launch traced here: 1550 us
  blocking collectives  1250 us (80%)
  local copies, waits for them, and re-layouts  140 us (9%)
  starting transfers between devices  85.2 us (5%)
  other arithmetic  50.4 us (3%)
    psum x3, blocking collectives, apply_tilde(): coarse_load = lax.psum(partial_load, ('grp', 'sub'))  571 us
    all_gather x3, blocking collectives, apply_tilde(): lax.all_gather(owned_values, ('grp', 'sub'), axis=1, tiled=True)  361 us
    psum x2, blocking collectives, per_device(): inner_now = lax.psum(jnp.sum(residual * precond, axis=1), ('grp', 'sub'))  209 us
    psum x1, blocking collectives, per_device(): curvature = lax.psum(jnp.sum(search * image, axis=1), ('grp', 'sub'))  107 us
    all_to_all x5, starting transfers between devices, partner(): lax.all_to_all(outgoing, 'sub', split_axis=1, concat_axis=1, tiled=True)  41.3 us
  transfers between devices with their start and end apart: 15, of which 4 were waited for; matrix products, arithmetic and copies ran while one was open for 2% of the time, Pallas kernels for 0%

commit v1 on v0

--- a/solution.py
+++ b/solution.py
@@ -96,7 +96,10 @@
             coarse_inverse,
             preferred_element_type=jnp.float32,
         )
-        coarse_values = lax.all_gather(owned_values, ("grp", "sub"), axis=1, tiled=True)
+        size = lax.axis_size(("grp", "sub"))
+        pieces = jnp.stack([owned_values for _ in range(size)])
+        pieces = lax.all_to_all(pieces, ("grp", "sub"), split_axis=0, concat_axis=0)
+        coarse_values = jnp.concatenate(pieces, axis=1)
         at_corners = (
             jnp.take(coarse_values, corner_index, axis=1)
             .astype(jnp.bfloat16)

time: 1560 us -> 1340 us (0.86)
  blocking collectives: 1250 us -> 972 us
  waiting for transfers between devices: 14.4 us -> 64.4 us
  local copies, waits for them, and re-layouts: 140 us -> 163 us
  starting transfers between devices: 85.2 us -> 63.7 us
    all_gather x3 -> x0, blocking collectives: 361 us -> none  [apply_tilde(): lax.all_gather(owned_values, ('grp', 'sub'), axis=1, tiled=True)]
    all_to_all x0 -> x2, blocking collectives: none -> 102 us  [apply_tilde(): pieces = lax.all_to_all(pieces, ('grp', 'sub'), split_axis=0, concat_axis=0)]
    all_to_all x0 -> x1, waiting for transfers between devices: none -> 34.4 us  [apply_tilde(): pieces = lax.all_to_all(pieces, ('grp', 'sub'), split_axis=0, concat_axis=0)]
    all_to_all x5, waiting for transfers between devices: 13.4 us -> 30 us  [partner(): lax.all_to_all(outgoing, 'sub', split_axis=1, concat_axis=1, tiled=True)]
    ppermute x5, starting transfers between devices: 30.1 us -> 14 us  [extended(): lax.ppermute(tail, axis, [(i, (i + 1) % count) for i in range(ends)])]
    all_to_all x5, starting transfers between devices: 41.3 us -> 25.4 us  [partner(): lax.all_to_all(outgoing, 'sub', split_axis=1, concat_axis=1, tiled=True)]
    unnamed x87 -> x86, local copies, waits for them, and re-layouts: 25.7 us -> 33.2 us
  transfers between devices with their start and end apart: 15 -> 16, of which waited for: 4 -> 6; matrix products, arithmetic and copies ran while one was open for 2% -> 2% of each run, Pallas kernels for 0% -> 0%
where the time goes in v1:
time: 1340 us; the launch traced here: 1330 us
  blocking collectives  972 us (73%)
  local copies, waits for them, and re-layouts  163 us (12%)
  waiting for transfers between devices  64.4 us (5%)
  starting transfers between devices  63.7 us (5%)
  other arithmetic  50.6 us (4%)
  matrix products  13.4 us (1%)
    psum x3, blocking collectives, apply_tilde(): coarse_load = lax.psum(partial_load, ('grp', 'sub'))  569 us
    psum x2, blocking collectives, per_device(): inner_now = lax.psum(jnp.sum(residual * precond, axis=1), ('grp', 'sub'))  201 us
    all_to_all x2, blocking collectives, apply_tilde(): pieces = lax.all_to_all(pieces, ('grp', 'sub'), split_axis=0, concat_axis=0)  102 us
    psum x1, blocking collectives, per_device(): curvature = lax.psum(jnp.sum(search * image, axis=1), ('grp', 'sub'))  100 us
    all_to_all x1, waiting for transfers between devices, apply_tilde(): pieces = lax.all_to_all(pieces, ('grp', 'sub'), split_axis=0, concat_axis=0)  34.4 us
    unnamed x86, local copies, waits for them, and re-layouts  33.2 us
    all_to_all x5, waiting for transfers between devices, partner(): lax.all_to_all(outgoing, 'sub', split_axis=1, concat_axis=1, tiled=True)  30 us
    gather x10, local copies, waits for them, and re-layouts, partner(): return jnp.take(joined, slot_inverse, axis=1)  27.3 us
  transfers between devices with their start and end apart: 16, of which 6 were waited for; matrix products, arithmetic and copies ran while one was open for 2% of the time, Pallas kernels for 0%

profile of v1, /device:TPU:1, one launch (start us, length us, event | category | flops | bytes accessed | tf_op | source)
XLA Modules:
  0.0 1329.5 jit_solution(8438843050691314655)
XLA Ops:
  4.8 6.2 scatter_custom_fusion
  11.1 2.0 fusion.112
  13.1 4.5 fusion.93
  17.6 6.9 fusion.91
  24.5 8.4 gather_fusion
  37.8 4.0 scatter_custom_fusion.1
  41.8 195.8 %all-reduce.4 = bf16[16,12288]{0,1:T(8,128)(2,1)} all-reduce(f32[16,12288]{0,1:T(8,128)} %scatter_custom_fusion.1), channel_id=1, replica_groups=mesh['grp'=32,'sub'=16] {'grp','sub'}, use_global_device_ids=true, to_apply=%region_2.3 | all-reduce | flops 196608 | bytes 1179648 | tf_op jit(solution)/shard_map/psum | solution.py:92
  237.6 2.8 fusion.120
  242.1 4.4 reshape.786
  246.5 14.1 %all-to-all-start = ((bf16[512,2,192]{2,1,0:T(2,128)(2,1)}), bf16[512,2,192]{2,1,0:T(2,128)(2,1)S(1)}, u32[]{:S(2)}, u32[]{:S(2)}) async-start(bf16[512,2,192]{2,1,0:T(2,128)(2,1)} %reshape.786), calls=%async_computation | async-start | bytes 1048576 | tf_op jit(solution)/shard_map/all_to_all | solution.py:101
  261.6 34.4 %all-to-all-done = bf16[512,2,192]{2,1,0:T(2,128)(2,1)S(1)} async-done(((bf16[512,2,192]{2,1,0:T(2,128)(2,1)}), bf16[512,2,192]{2,1,0:T(2,128)(2,1)S(1)}, u32[]{:S(2)}, u32[]{:S(2)}) %all-to-all-start) | async-done | bytes 393248 | tf_op jit(solution)/shard_map/all_to_all | solution.py:101
  296.0 2.7 reshape.787
  298.6 4.5 copy.259
  303.1 2.9 gather_fusion.2
  308.8 4.0 gather_fusion.3
  317.5 3.5 all-to-all-start.1
  322.3 2.5 collective-permute-start
  324.8 1.9 collective-permute-start.1
  327.5 5.2 all-to-all-done.1
  339.8 4.8 gather_fusion.5
  348.3 2.8 gather_fusion.7
  351.1 5.1 gather_fusion.6
  361.5 6.6 all-to-all-start.2
  368.7 3.9 collective-permute-start.2
  374.5 5.9 all-to-all-done.2
  387.1 4.8 gather_fusion.8
  391.9 2.0 copy.277
  395.2 4.0 scatter_custom_fusion.2
  399.2 188.0 %all-reduce.5 = bf16[16,12288]{0,1:T(8,128)(2,1)} all-reduce(f32[16,12288]{0,1:T(8,128)} %scatter_custom_fusion.2), channel_id=1, replica_groups=mesh['grp'=32,'sub'=16] {'grp','sub'}, use_global_device_ids=true, to_apply=%region_6.11 | all-reduce | flops 196608 | bytes 1179648 | tf_op jit(solution)/shard_map/psum | solution.py:92
  587.2 3.0 fusion.119
  591.8 4.4 reshape.792
  596.1 49.9 %all_to_all.40 = bf16[512,2,192]{2,1,0:T(2,128)(2,1)} all-to-all(bf16[512,2,192]{2,1,0:T(2,128)(2,1)} %reshape.792), channel_id=1, replica_groups=mesh['grp'=32,'sub'=16] {'grp','sub'}, dimensions={0} | all-to-all | bytes 786432 | tf_op jit(solution)/shard_map/all_to_all | solution.py:101
  646.0 4.2 reshape.793
  650.2 4.5 copy.282
  654.7 3.0 gather_fusion.9
  659.7 2.8 gather_fusion.11
  662.5 5.1 gather_fusion.10
  672.9 3.5 all-to-all-start.4
  677.7 2.4 collective-permute-start.4
  680.1 2.5 collective-permute-start.5
  682.6 5.4 all-to-all-done.4
  694.7 5.1 gather_fusion.12
  702.3 99.4 %all-reduce = (f32[16]{0:T(128)S(1)}, f32[16]{0:T(128)S(1)}) all-reduce(f32[16]{0:T(128)S(1)} %get-tuple-element.15, f32[16]{0:T(128)S(1)} %get-tuple-element.14), channel_id=1, replica_groups=mesh['grp'=32,'sub'=16] {'grp','sub'}, use_global_device_ids=true, to_apply=%region_4.9 | all-reduce | flops 32 | bytes 256 | tf_op jit(solution)/shard_map/psum | solution.py:134
  805.8 2.8 gather_fusion.13
  810.6 8.2 all-to-all-start.5
  819.5 2.7 collective-permute-start.6
  822.2 1.9 collective-permute-start.7
  824.1 6.3 all-to-all-done.5
  831.8 3.7 gather_fusion.15
  836.9 101.9 %psum.53 = f32[16]{0:T(128)S(1)} all-reduce(f32[16]{0:T(128)S(1)} %multiply_reduce_fusion.1), channel_id=1, replica_groups=mesh['grp'=32,'sub'=16] {'grp','sub'}, use_global_device_ids=true, to_apply=%region_10.15 | all-reduce | flops 16 | bytes 128 | tf_op jit(solution)/shard_map/psum | solution.py:134
  939.9 4.0 scatter_custom_fusion.3
  943.8 185.1 %all-reduce.6 = bf16[16,12288]{0,1:T(8,128)(2,1)} all-reduce(f32[16,12288]{0,1:T(8,128)} %scatter_custom_fusion.3), channel_id=1, replica_groups=mesh['grp'=32,'sub'=16] {'grp','sub'}, use_global_device_ids=true, to_apply=%region_12.17 | all-reduce | flops 196608 | bytes 1179648 | tf_op jit(solution)/shard_map/psum | solution.py:92
  1129.0 2.8 fusion.118
  1133.4 3.7 reshape.798
  1137.1 52.0 %all_to_all.41 = bf16[512,2,192]{2,1,0:T(2,128)(2,1)S(1)} all-to-all(bf16[512,2,192]{2,1,0:T(2,128)(2,1)S(1)} %reshape.798), channel_id=1, replica_groups=mesh['grp'=32,'sub'=16] {'grp','sub'}, dimensions={0} | all-to-all | bytes 786432 | tf_op jit(solution)/shard_map/all_to_all | solution.py:101
  1189.1 2.7 reshape.799
  1191.7 4.5 copy.305
  1196.2 3.0 gather_fusion.16
  1202.0 2.8 gather_fusion.17
  1206.8 3.5 all-to-all-start.7
  1210.4 2.5 collective-permute-start.8
  1214.8 7.2 all-to-all-done.7
  1223.3 2.6 gather_fusion.19
  1227.2 100.5 %psum.55 = f32[16]{0:T(128)S(1)} all-reduce(f32[16]{0:T(128)S(1)} %multiply_reduce_fusion), channel_id=1, replica_groups=mesh['grp'=32,'sub'=16] {'grp','sub'}, use_global_device_ids=true, to_apply=%region_14.19 | all-reduce | flops 16 | bytes 128 | tf_op jit(solution)/shard_map/psum | solution.py:141
  (240 shorter events, 90.0 us)
Async XLA Ops:
  0.6 305.7 %copy-start = (bf16[1,1,3,512,512]{4,3,2,1,0:T(8,128)(2,1)S(1)}, bf16[1,1,3,512,512]{4,3,2,1,0:T(8,128)(2,1)}, u32[]{:S(2)}) copy-start(bf16[1,1,3,512,512]{4,3,2,1,0:T(8,128)(2,1)} %param.23) | copy-start | bytes 4718596
  11.0 6.6 copy-start.16
  11.1 376.0 %copy-start.8 = (s32[2048]{0:T(1024)}, s32[2048]{0:T(1024)S(1)}, u32[]{:S(2)}) copy-start(s32[2048]{0:T(1024)S(1)} %pad_clamp_fusion) | copy-start | bytes 24580
  24.5 8.4 copy-start.21
  24.5 13.0 copy-start.4
  41.8 195.8 %copy-start.2 = (bf16[24,12288]{1,0:T(8,128)(2,1)S(1)}, bf16[24,12288]{1,0:T(8,128)(2,1)}, u32[]{:S(2)}) copy-start(bf16[24,12288]{1,0:T(8,128)(2,1)} %param.27) | copy-start | bytes 1769476
  240.5 20.1 %copy-start.23 = (s32[1,1,1536]{2,1,0:T(1,128)S(1)}, s32[1,1,1536]{2,1,0:T(1,128)}, u32[]{:S(2)}) copy-start(s32[1,1,1536]{2,1,0:T(1,128)} %param.29) | copy-start | bytes 18436
  246.5 49.5 %all-to-all-start = ((bf16[512,2,192]{2,1,0:T(2,128)(2,1)}), bf16[512,2,192]{2,1,0:T(2,128)(2,1)S(1)}, u32[]{:S(2)}, u32[]{:S(2)}) async-start(bf16[512,2,192]{2,1,0:T(2,128)(2,1)} %reshape.786), calls=%async_computation | async-start | bytes 1048576 | tf_op jit(solution)/shard_map/all_to_all | solution.py:101
  260.9 46.2 %copy-start.17 = (s32[1024]{0:T(1024)}, s32[1024]{0:T(1024)S(1)}, u32[]{:S(2)}) copy-start(s32[1024]{0:T(1024)S(1)} %pad_clamp_fusion.1) | copy-start | bytes 12292
  261.0 42.2 %copy-start.24 = (s32[1024]{0:T(1024)}, s32[1024]{0:T(1024)S(1)}, u32[]{:S(2)}) copy-start(s32[1024]{0:T(1024)S(1)} %pad_clamp_fusion.2) | copy-start | bytes 12292
  261.0 45.1 %copy-start.25 = (pred[72]{0:T(512)(128)(4,1)}, pred[72]{0:T(512)(128)(4,1)S(1)}, u32[]{:S(2)}) copy-start(pred[72]{0:T(512)(128)(4,1)S(1)} %compare_and_fusion.3) | copy-start | bytes 220
  261.6 400.9 %copy-start.6 = (s32[1024]{0:T(1024)}, s32[1024]{0:T(1024)S(1)}, u32[]{:S(2)}) copy-start(s32[1024]{0:T(1024)S(1)} %broadcast_clamp_fusion) | copy-start | bytes 12292
  261.6 95.8 %copy-start.14 = (pred[16,64]{1,0:T(8,128)(4,1)}, pred[16,64]{1,0:T(8,128)(4,1)S(1)}, u32[]{:S(2)}) copy-start(pred[16,64]{1,0:T(8,128)(4,1)S(1)} %compare_and_fusion.1) | copy-start | bytes 3076
  312.8 33.9 %copy-start.1 = (bf16[1,1,3,512,512]{4,3,2,1,0:T(8,128)(2,1)S(1)}, bf16[1,1,3,512,512]{4,3,2,1,0:T(8,128)(2,1)}, u32[]{:S(2)}) copy-start(bf16[1,1,3,512,512]{4,3,2,1,0:T(8,128)(2,1)} %param.24) | copy-start | bytes 4718596
  317.5 15.2 %all-to-all-start.1 = ((f32[16,1,1024]{2,1,0:T(1,128)}), f32[16,1,1024]{2,1,0:T(1,128)S(1)}, u32[]{:S(2)}, u32[]{:S(2)}) async-start(f32[16,1,1024]{2,1,0:T(1,128)} %reshape.788), calls=%async_computation.1 | async-start | bytes 131072 | tf_op jit(solution)/shard_map/all_to_all | solution.py:71
  322.3 15.5 %collective-permute-start = (f32[16,1,256]{2,0,1:T(8,128)}, f32[16,1,256]{2,0,1:T(8,128)S(1)}, u32[]{:S(2)}, u32[]{:S(2)}) collective-permute-start(f32[16,1,256]{2,0,1:T(8,128)} %get-tuple-element.34), channel_id=1, source_target_pairs={{0,16},{16,32},{32,48},{48,64},{64,80},{80,96},{96,112},{112,128},... | collective-permute-start | bytes 49160 | tf_op jit(solution)/shard_map/ppermute | solution.py:22
  324.8 13.0 collective-permute-start.1
  327.5 66.5 %copy-start.10 = (pred[1536]{0:T(1024)(128)(4,1)}, pred[1536]{0:T(1024)(128)(4,1)S(1)}, u32[]{:S(2)}) copy-start(pred[1536]{0:T(1024)(128)(4,1)S(1)} %compare_and_fusion) | copy-start | bytes 4612
  336.2 12.2 copy-start.18
  361.5 19.0 %all-to-all-start.2 = ((f32[16,1,1024]{2,1,0:T(1,128)}), f32[16,1,1024]{2,1,0:T(1,128)S(1)}, u32[]{:S(2)}, u32[]{:S(2)}) async-start(f32[16,1,1024]{2,1,0:T(1,128)} %reshape.790), calls=%async_computation.2 | async-start | bytes 131072 | tf_op jit(solution)/shard_map/all_to_all | solution.py:71
  368.7 16.4 %collective-permute-start.2 = (f32[16,1,256]{2,0,1:T(8,128)}, f32[16,1,256]{2,0,1:T(8,128)S(1)}, u32[]{:S(2)}, u32[]{:S(2)}) collective-permute-start(f32[16,1,256]{2,0,1:T(8,128)} %get-tuple-element.32), channel_id=1, source_target_pairs={{0,16},{16,32},{32,48},{48,64},{64,80},{80,96},{96,112},{112,128},... | collective-permute-start | bytes 49160 | tf_op jit(solution)/shard_map/ppermute | solution.py:22
  372.6 12.5 collective-permute-start.3
  374.5 24.6 %copy-start.12 = (f32[1536]{0:T(1024)}, f32[1536]{0:T(1024)S(1)}, u32[]{:S(2)}) copy-start(f32[1536]{0:T(1024)S(1)} %broadcast_multiply_fusion) | copy-start | bytes 18436
  650.2 7.5 copy-start.26
  650.2 9.5 copy-start.19
  672.9 15.2 %all-to-all-start.4 = ((f32[16,1,1024]{2,1,0:T(1,128)}), f32[16,1,1024]{2,1,0:T(1,128)S(1)}, u32[]{:S(2)}, u32[]{:S(2)}) async-start(f32[16,1,1024]{2,1,0:T(1,128)} %reshape.794), calls=%async_computation.4 | async-start | bytes 131072 | tf_op jit(solution)/shard_map/all_to_all | solution.py:71
  677.7 15.0 %collective-permute-start.4 = (f32[16,1,256]{2,0,1:T(8,128)}, f32[16,1,256]{2,0,1:T(8,128)}, u32[]{:S(2)}, u32[]{:S(2)}) collective-permute-start(f32[16,1,256]{2,0,1:T(8,128)} %get-tuple-element.30), channel_id=1, source_target_pairs={{0,16},{16,32},{32,48},{48,64},{64,80},{80,96},{96,112},{112,128},... | collective-permute-start | bytes 49160 | tf_op jit(solution)/shard_map/ppermute | solution.py:22
  680.1 12.6 collective-permute-start.5
  691.0 110.6 %copy-start.11 = (pred[1536]{0:T(1024)(128)(4,1)S(1)}, pred[1536]{0:T(1024)(128)(4,1)}, u32[]{:S(2)}) copy-start(pred[1536]{0:T(1024)(128)(4,1)} %copy-done.10) | copy-start | bytes 4612
  693.5 110.5 %copy-start.20 = (s32[1024]{0:T(1024)S(1)}, s32[1024]{0:T(1024)}, u32[]{:S(2)}) copy-start(s32[1024]{0:T(1024)} %copy-done.17) | copy-start | bytes 12292
  693.6 112.2 %copy-start.7 = (s32[1024]{0:T(1024)S(1)}, s32[1024]{0:T(1024)}, u32[]{:S(2)}) copy-start(s32[1024]{0:T(1024)} %copy-done.6) | copy-start | bytes 12292
  699.8 108.9 %copy-start.15 = (pred[16,64]{1,0:T(8,128)(4,1)S(1)}, pred[16,64]{1,0:T(8,128)(4,1)}, u32[]{:S(2)}) copy-start(pred[16,64]{1,0:T(8,128)(4,1)} %copy-done.14) | copy-start | bytes 3076
  801.6 2.4 copy-start.32
  801.6 1.6 copy-start.28
  803.8 28.0 %copy-start.9 = (s32[2048]{0:T(1024)S(1)}, s32[2048]{0:T(1024)}, u32[]{:S(2)}) copy-start(s32[2048]{0:T(1024)} %copy-done.8) | copy-start | bytes 24580
  805.7 31.0 %copy-start.5 = (f32[16,1536]{1,0:T(8,128)S(1)}, f32[16,1536]{1,0:T(8,128)}, u32[]{:S(2)}) copy-start(f32[16,1536]{1,0:T(8,128)} %get-tuple-element.21) | copy-start | bytes 294916
  805.7 31.0 %copy-start.13 = (f32[1536]{0:T(1024)S(1)}, f32[1536]{0:T(1024)}, u32[]{:S(2)}) copy-start(f32[1536]{0:T(1024)} %copy-done.12) | copy-start | bytes 18436
  805.8 133.1 %copy-start.33 = (f32[16]{0:T(128)S(1)}, f32[16]{0:T(128)}, u32[]{:S(2)}) copy-start(f32[16]{0:T(128)} %copy-done.32) | copy-start | bytes 196
  810.6 19.8 %all-to-all-start.5 = ((f32[16,1,1024]{2,1,0:T(1,128)}), f32[16,1,1024]{2,1,0:T(1,128)S(1)}, u32[]{:S(2)}, u32[]{:S(2)}) async-start(f32[16,1,1024]{2,1,0:T(1,128)} %reshape.796), calls=%async_computation.5 | async-start | bytes 131072 | tf_op jit(solution)/shard_map/all_to_all | solution.py:71
  819.5 11.9 collective-permute-start.6
  822.2 9.2 collective-permute-start.7
  938.8 5.0 copy-start.30
  943.8 185.1 %copy-start.3 = (bf16[24,12288]{1,0:T(8,128)(2,1)S(1)}, bf16[24,12288]{1,0:T(8,128)(2,1)}, u32[]{:S(2)}) copy-start(bf16[24,12288]{1,0:T(8,128)(2,1)} %param.27) | copy-start | bytes 1769476
  1191.7 7.5 copy-start.27
  1196.2 14.1 %copy-start.22 = (pred[2,256]{1,0:T(4,128)(4,1)S(1)}, pred[2,256]{1,0:T(4,128)(4,1)}, u32[]{:S(2)}) copy-start(pred[2,256]{1,0:T(4,128)(4,1)} %compare_and_fusion.2) | copy-start | bytes 1540
  1202.0 125.6 %copy-start.31 = (f32[16]{0:T(128)S(1)}, f32[16]{0:T(128)}, u32[]{:S(2)}) copy-start(f32[16]{0:T(128)} %copy-done.30) | copy-start | bytes 196
  1202.0 125.6 %copy-start.29 = (f32[16]{0:T(128)S(1)}, f32[16]{0:T(128)}, u32[]{:S(2)}) copy-start(f32[16]{0:T(128)} %copy-done.28) | copy-start | bytes 196
  1206.8 15.2 %all-to-all-start.7 = ((f32[16,1,1024]{2,1,0:T(1,128)}), f32[16,1,1024]{2,1,0:T(1,128)S(1)}, u32[]{:S(2)}, u32[]{:S(2)}) async-start(f32[16,1,1024]{2,1,0:T(1,128)} %reshape.800), calls=%async_computation.7 | async-start | bytes 131072 | tf_op jit(solution)/shard_map/all_to_all | solution.py:71
  1210.4 12.6 collective-permute-start.8
  1212.9 10.1 collective-permute-start.9
